TPU v7x, 512 devices: a whole 4x4x16 slice. The times are simulated.
512 devices in a mesh: dp: 32 (over x, z_hi, core), tensor: 16 (over z_lo, y).
Axes of the slice: x: 4, y: 4, z: 16 (z_hi: 4, z_lo: 4; z = z_hi * 4 + z_lo), core: 2. Of those that a mesh axis runs over, the one named last changes fastest.
Arguments:
- activations: bfloat16 [640, 26624], P('dp', 'tensor'), may hold values from -6 to 6
- weight_codes: int32 [26624, 8192], P(('tensor', 'dp')), may hold values from 0 to 15
- scale_index: int32 [26624, 64], P(('tensor', 'dp')), may hold values from 0 to 15, as said below
- scale_table: float32 [16], replicated
- bit_widths: int32 [1, 26624, 64], P(None, ('tensor', 'dp')), may hold values from 2 to 4
Outputs:
- base_output: bfloat16 [640, 8192], P('tensor', 'dp')
- scores: float32 [1, 640], P(None, 'tensor')
Inputs may be any that keep to these rules, and one draw needn't show every extreme that they name: `scale_index`: an entry of scale_table for each row and each group of 128 columns.
All inputs are finite; a program needn't handle non-finite values.
Results may differ from a plain program's by a relative error of at most 0.0058.
Values may be sent and summed in bfloat16 or wider, within the bound.
No kernel may reach another device: no remote copies, remote signals or barrier semaphores. Data moves between devices by JAX's collectives and lax.ppermute only.
A program may use at most 64 MiB of HBM per device.

v0:
```python
import math
import jax
import jax.numpy as jnp
from jax import lax
from jax.sharding import PartitionSpec as P

HB = 128
NCAND = 1
score_divisor = 512.0


def side_by_side(arrays, axis, split_dim, concat_dim, along):
    columns = [a.reshape(*a.shape[:along], -1) for a in arrays]
    both = jnp.concatenate(columns, axis=along)
    whole, at, done = (
        lax.all_to_all(both, axis, split_axis=split_dim, concat_axis=concat_dim, tiled=True),
        0,
        [],
    )
    for a, column in zip(arrays, columns):
        piece = whole[..., at : at + column.shape[along]]
        done.append(piece.reshape(*piece.shape[:along], *a.shape[along:]))
        at += column.shape[along]
    return tuple(done)


def split_up(value, dim, size):
    before, after = (value.shape[:dim], value.shape[dim + 1 :])
    return jnp.moveaxis(value.reshape(*before, size, -1, *after), dim, 0)


def sum_at_owner(value, axis, dim):
    size = lax.axis_size(axis)
    tiles = lax.all_to_all(split_up(value, dim, size), axis, 0, 0, tiled=True)
    return jnp.sum(tiles, axis=0)


def from_everyone(value, axis):
    size = lax.axis_size(axis)
    return lax.all_to_all(
        jnp.broadcast_to(value[None], (size, *value.shape)), axis, 0, 0, tiled=True
    )


def over_copies(value, axis):
    return from_everyone(value, axis).sum(axis=0)


def sylvester(order_size):
    positions = jnp.arange(order_size, dtype=jnp.int32)
    intersection = positions[:, None] & positions[None, :]
    parity = jnp.zeros((order_size, order_size), jnp.int32)
    for shift_bit in range(max(order_size.bit_length() - 1, 0)):
        parity = parity + (intersection >> shift_bit & 1)
    parity = parity % 2
    return (1 - 2 * parity).astype(jnp.float32)


def dequantize(grouped, index_rows, scale_table, bits_rows):
    one_hot = (index_rows[..., None] == jnp.arange(scale_table.shape[0], dtype=jnp.int32)).astype(
        jnp.float32
    )
    scales = jnp.sum(one_hot * scale_table, axis=-1)
    base_w = ((grouped - 8).astype(jnp.float32) * scales[..., None]).astype(jnp.bfloat16)
    step_size = jnp.where(bits_rows == 2, 4, jnp.where(bits_rows == 3, 2, 1)).astype(jnp.int32)[
        ..., None
    ]
    cand_codes = grouped[None] // step_size * step_size + step_size // 2
    cand_w = ((cand_codes - 8).astype(jnp.float32) * scales[None, :, :, None]).astype(jnp.bfloat16)
    row_count = grouped.shape[0]
    col_count = grouped.shape[1] * grouped.shape[2]
    return jnp.concatenate([base_w[None], cand_w], axis=0).reshape(NCAND + 1, row_count, col_count)


def local(activations, weight_codes, scale_index, scale_table, bit_widths):
    tensor_size = lax.axis_size("tensor")
    tok_rows, feat_width = activations.shape
    block_signs = sylvester(HB).astype(jnp.bfloat16)
    blocked = jnp.einsum(
        "rnb,bc->rnc",
        activations.reshape(tok_rows, feat_width // HB, HB),
        block_signs,
        preferred_element_type=jnp.float32,
    ).reshape(tok_rows, feat_width)
    sign_matrix = sylvester(tensor_size)
    shaped = blocked.reshape(tok_rows, tensor_size, feat_width // tensor_size)
    spread = jnp.einsum(
        "js,rsc->rjc",
        sign_matrix,
        lax.all_to_all(shaped, "tensor", split_axis=1, concat_axis=1, tiled=True),
        precision=lax.Precision.HIGHEST,
    )
    mixed_rows = lax.all_to_all(spread, "tensor", split_axis=1, concat_axis=1, tiled=True).reshape(
        tok_rows, feat_width
    )
    rotated = (mixed_rows * (1.0 / math.sqrt(HB * tensor_size))).astype(jnp.bfloat16)
    all_tokens = lax.all_gather(rotated, "dp", axis=0, tiled=True)
    store_rows, model_width = weight_codes.shape
    group_count = scale_index.shape[1]
    group_width = model_width // group_count
    code_wire = weight_codes.reshape(store_rows, group_count, group_width).astype(jnp.bfloat16)
    index_wire = scale_index.astype(jnp.bfloat16)
    bits_wire = jnp.transpose(bit_widths, (1, 2, 0)).astype(jnp.bfloat16)
    code_home, index_home, bits_home = side_by_side(
        (code_wire, index_wire, bits_wire), "dp", 1, 0, 2
    )
    local_grouped = code_home.astype(jnp.int32)
    local_index = index_home.astype(jnp.int32)
    local_bits = jnp.transpose(bits_home.astype(jnp.int32), (2, 0, 1))
    local_weights = dequantize(local_grouped, local_index, scale_table, local_bits)
    token_sums = sum_at_owner(
        jnp.einsum("tf,kfd->tkd", all_tokens, local_weights, preferred_element_type=jnp.float32),
        "tensor",
        0,
    )
    token_sums = jnp.transpose(token_sums, (1, 0, 2))
    base_rows = token_sums[0]
    cand_diffs = token_sums[1:] - base_rows[None]
    block_scores = jnp.sum(cand_diffs * cand_diffs, axis=2) / score_divisor
    scores = over_copies(block_scores, "dp")
    return (base_rows.astype(jnp.bfloat16), scores)


def solution(mesh):
    in_specs = (
        P("dp", "tensor"),
        P(("tensor", "dp"), None),
        P(("tensor", "dp"), None),
        P(),
        P(None, ("tensor", "dp"), None),
    )
    out_specs = (P("tensor", "dp"), P(None, "tensor"))
    return jax.shard_map(local, mesh=mesh, in_specs=in_specs, out_specs=out_specs, check_vma=False)
```

profile of v0, /device:TPU:1, one launch (start us, length us, event | category | flops | bytes accessed | tf_op | source)
XLA Modules:
  0.0 236.9 jit_solution(8731852525822146054)
XLA Ops:
  7.2 0.0 copy-start.2
  7.2 1.0 reshape.173
  8.1 0.2 convolution_bitcast_fusion.1
  8.4 0.0 copy-start.1
  8.4 0.2 reshape_reshape.3
  8.6 0.1 copy.92
  8.7 0.0 copy-start
  8.7 17.6 %all_to_all.38 = f32[20,16,104]{2,0,1:T(8,128)S(1)} all-to-all(f32[20,16,104]{2,0,1:T(8,128)S(1)} %copy.92), channel_id=1, replica_groups=mesh['dp'=32,'tensor'=16] {'tensor'}, dimensions={1} | all-to-all | bytes 266240 | tf_op jit(solution)/shard_map/all_to_all | solution.py:90
  26.3 0.3 convolution_bitcast_fusion
  26.6 0.7 copy.94
  27.3 4.4 %all-to-all-start.1 = ((f32[20,16,104]{2,0,1:T(8,128)}), f32[20,16,104]{2,0,1:T(8,128)}, u32[]{:S(2)}, u32[]{:S(2)}) async-start(f32[20,16,104]{2,0,1:T(8,128)} %copy.94), calls=%async_computation.1 | async-start | bytes 393216 | tf_op jit(solution)/shard_map/all_to_all | solution.py:93
  31.8 0.0 copy-done.2
  31.8 0.5 copy.98
  32.3 0.0 copy-done.1
  32.3 0.5 copy.97
  32.8 0.1 convert_element_type.72
  32.9 0.2 copy.111
  33.2 0.1 slice.25
  33.2 0.5 pad_maximum_fusion
  33.8 1.0 copy.133
  34.8 3.5 %reshape.185 = bf16[32,2,6760]{2,1,0:T(2,128)(2,1)} reshape(bf16[64,52,130]{2,1,0:T(8,128)(2,1)S(1)} %bitcast.52) | data formatting | bytes 1730560
  38.3 1.8 all-to-all-done.1
  40.1 18.0 %all-to-all-start.2 = ((bf16[32,2,6760]{2,1,0:T(2,128)(2,1)}), bf16[32,2,6760]{2,1,0:T(2,128)(2,1)S(1)}, u32[]{:S(2)}, u32[]{:S(2)}) async-start(bf16[32,2,6760]{2,1,0:T(2,128)(2,1)} %reshape.185), calls=%async_computation.2 | async-start | bytes 1736704 | tf_op jit(solution)/shard_map/all_to_all | solution.py:16
  58.1 0.0 all-gather.3.cloned.1.call-start
  58.2 1.0 fusion.16
  59.1 0.8 reshape.176
  59.9 0.0 all-gather.3.cloned.1.call-update
  59.9 44.8 %all-to-all-done.2 = bf16[32,2,6760]{2,1,0:T(2,128)(2,1)S(1)} async-done(((bf16[32,2,6760]{2,1,0:T(2,128)(2,1)}), bf16[32,2,6760]{2,1,0:T(2,128)(2,1)S(1)}, u32[]{:S(2)}, u32[]{:S(2)}) %all-to-all-start.2) | async-done | bytes 865312 | tf_op jit(solution)/shard_map/all_to_all | solution.py:16
  104.8 3.2 %reshape.186 = bf16[64,52,130]{2,1,0:T(8,128)(2,1)S(1)} reshape(bf16[32,2,6760]{2,1,0:T(2,128)(2,1)S(1)} %all-to-all-done.2) | data formatting | bytes 1730560
  108.0 3.1 %copy.130 = bf16[52,32,2,130]{3,2,1,0:T(2,128)(2,1)} copy(bf16[52,32,2,130]{3,0,2,1:T(8,128)(2,1)S(1)} %bitcast.53) | data formatting | bytes 1730560 | tf_op jit(solution)/shard_map/all_to_all | solution.py:16
  111.1 6.1 %copy.101 = bf16[32,52,2,130]{1,0,3,2:T(8,128)(2,1)S(1)} copy(bf16[32,52,2,130]{3,2,0,1:T(2,128)(2,1)} %bitcast.54) | data formatting | bytes 1730560 | tf_op jit(solution)/shard_map/all_to_all | solution.py:16
  117.2 0.0 copy-start.3
  117.2 4.2 %all_to_all.30 = bf16[1664,2,130]{0,2,1:T(8,128)(2,1)S(1)} reshape(bf16[32,52,2,130]{1,0,3,2:T(8,128)(2,1)S(1)} %copy.101) | data formatting | bytes 1730560 | tf_op jit(solution)/shard_map/all_to_all | solution.py:16
  121.5 0.1 select_reduce_fusion
  121.6 17.6 %fusion.10 = (bf16[1664,2,128]{0,2,1:T(8,128)(2,1)S(1)}, bf16[1664,2,128]{0,2,1:T(8,128)(2,1)S(1)}) fusion(f32[1664,2]{0,1:T(2,128)S(1)} %select_reduce_fusion, bf16[1664,2,130]{0,2,1:T(8,128)(2,1)S(1)} %all_to_all.30, s32[1664,2]{0,1:T(2,128)S(1)} %get-tuple-element.5, s32[1664,2]{0,1:T(2,128)S(1)} %bitcast.62, s32[1664,2]{0,1:T(2,128)S(1)} %get-tuple-element.4), kind=kLoop, calls=%fused_computation.15 | loop fusion | flops 8093696 | bytes 2609152 | tf_op jit(solution)/shard_map/convert_element_type | solution.py:64
  139.2 0.6 copy.107
  139.8 1.3 copy.108
  141.1 20.7 %all-gather.3.cloned.1.call-done = bf16[32,20,1664]{2,1,0:T(8,128)(2,1)} async-done(((bf16[1,20,1664]{2,1,0:T(8,128)(2,1)}), bf16[32,20,1664]{2,1,0:T(8,128)(2,1)}) %all-gather.3.cloned.1.call-update) | async-done | bytes 2129936 | tf_op jit(solution)/shard_map/all_gather | solution.py:97
  161.8 2.6 %reshape.182 = bf16[16,40,1664,1]{2,1,0,3:T(8,128)(2,1)S(1)} reshape(bf16[32,20,1664]{2,1,0:T(8,128)(2,1)} %all-gather.3.cloned.1.call-done) | data formatting | bytes 4259840 | tf_op jit(solution)/shard_map/tf,kfd->tkd/dot_general | solution.py:112
  164.4 2.5 %fusion = f32[16,40,2,256]{3,1,2,0:T(8,128)S(1)} fusion(bf16[16,40,1664,1]{2,1,0,3:T(8,128)(2,1)S(1)} %reshape.182, bf16[1,1664,256]{2,1,0:T(8,128)(2,1)} %copy.108, bf16[1,1664,256]{2,1,0:T(8,128)(2,1)S(1)} %copy.107), kind=kOutput, calls=%fused_computation.5 | convolution fusion | flops 1093926912 | bytes 5144576 | tf_op jit(solution)/shard_map/tf,kfd->tkd/dot_general | solution.py:112
  167.0 36.0 %all_to_all.39 = f32[16,40,2,256]{3,1,2,0:T(8,128)S(1)} all-to-all(f32[16,40,2,256]{3,1,2,0:T(8,128)S(1)} %fusion), channel_id=1, replica_groups=mesh['dp'=32,'tensor'=16] {'tensor'}, dimensions={0} | all-to-all | bytes 2621440 | tf_op jit(solution)/shard_map/all_to_all | solution.py:34
  203.0 0.1 reduce_sum.39
  203.1 0.1 fusion.25
  203.2 0.6 broadcast_in_dim.17
  203.8 11.5 %all-to-all-start.4 = ((f32[32,1,40]{2,1,0:T(1,128)}), f32[32,1,40]{2,1,0:T(1,128)S(1)}, u32[]{:S(2)}, u32[]{:S(2)}) async-start(f32[32,1,40]{2,1,0:T(1,128)} %broadcast_in_dim.17), calls=%async_computation.4 | async-start | bytes 32768 | tf_op jit(solution)/shard_map/all_to_all | solution.py:40
  215.4 0.6 fusion.35
  216.0 13.6 %all-to-all-done.4 = f32[32,1,40]{2,1,0:T(1,128)S(1)} async-done(((f32[32,1,40]{2,1,0:T(1,128)}), f32[32,1,40]{2,1,0:T(1,128)S(1)}, u32[]{:S(2)}, u32[]{:S(2)}) %all-to-all-start.4) | async-done | bytes 5152 | tf_op jit(solution)/shard_map/all_to_all | solution.py:40
  229.6 0.5 reduce_sum.41
  (11 shorter events, 0.1 us)
Async XLA Ops:
  7.2 24.6 %copy-start.2 = (s32[1,52,64]{2,0,1:T(1,128)S(1)}, s32[1,52,64]{2,0,1:T(1,128)}, u32[]{:S(2)}) copy-start(s32[1,52,64]{2,0,1:T(1,128)} %param.9) | copy-start | bytes 39940
  8.4 23.9 %copy-start.1 = (s32[52,64]{1,0:T(8,128)S(1)}, s32[52,64]{1,0:T(8,128)}, u32[]{:S(2)}) copy-start(s32[52,64]{1,0:T(8,128)} %param.7) | copy-start | bytes 39940
  8.7 24.1 %copy-start = (s32[52,8192]{1,0:T(8,128)S(1)}, s32[52,8192]{1,0:T(8,128)}, u32[]{:S(2)}) copy-start(s32[52,8192]{1,0:T(8,128)} %param.6) | copy-start | bytes 5111812
  27.3 12.8 %all-to-all-start.1 = ((f32[20,16,104]{2,0,1:T(8,128)}), f32[20,16,104]{2,0,1:T(8,128)}, u32[]{:S(2)}, u32[]{:S(2)}) async-start(f32[20,16,104]{2,0,1:T(8,128)} %copy.94), calls=%async_computation.1 | async-start | bytes 393216 | tf_op jit(solution)/shard_map/all_to_all | solution.py:93
  40.1 64.7 %all-to-all-start.2 = ((bf16[32,2,6760]{2,1,0:T(2,128)(2,1)}), bf16[32,2,6760]{2,1,0:T(2,128)(2,1)S(1)}, u32[]{:S(2)}, u32[]{:S(2)}) async-start(bf16[32,2,6760]{2,1,0:T(2,128)(2,1)} %reshape.185), calls=%async_computation.2 | async-start | bytes 1736704 | tf_op jit(solution)/shard_map/all_to_all | solution.py:16
  58.1 103.7 %all-gather.3.cloned.1.call-start = ((), (), s32[]{:S(2)}) async-start(), calls=%async_computation.5 | async-start | bytes 2635776 | tf_op jit(solution)/shard_map/all_gather | solution.py:97
  117.2 4.3 %copy-start.3 = (f32[16]{0:T(128)S(1)}, f32[16]{0:T(128)}, u32[]{:S(2)}) copy-start(f32[16]{0:T(128)} %param.8) | copy-start | bytes 196
  203.8 25.7 %all-to-all-start.4 = ((f32[32,1,40]{2,1,0:T(1,128)}), f32[32,1,40]{2,1,0:T(1,128)S(1)}, u32[]{:S(2)}, u32[]{:S(2)}) async-start(f32[32,1,40]{2,1,0:T(1,128)} %broadcast_in_dim.17), calls=%async_computation.4 | async-start | bytes 32768 | tf_op jit(solution)/shard_map/all_to_all | solution.py:40
Sparse Core Ops, SparseCore 0:
  62.0 99.7 all-gather.2
where the time goes:
time: 238 us; the launch traced here: 237 us
  waiting for transfers between devices  81 us (34%)
  blocking collectives  53.6 us (23%)
  starting transfers between devices  33.9 us (14%)
  local copies, waits for them, and re-layouts  30.9 us (13%)
  other arithmetic  20.1 us (8%)
  between operations  14.3 us (6%)
  matrix products  3.08 us (1%)
    all_to_all x1, waiting for transfers between devices, side_by_side(): lax.all_to_all(both, axis, split_axis=split_dim, concat_axis=concat_dim,...  44.8 us
    all_to_all x1, blocking collectives, sum_at_owner(): tiles = lax.all_to_all(split_up(value, dim, size), axis, 0, 0, tiled=True)  36 us
    all_gather x1, waiting for transfers between devices, local(): all_tokens = lax.all_gather(rotated, 'dp', axis=0, tiled=True)  20.7 us
    all_to_all x1, starting transfers between devices, side_by_side(): lax.all_to_all(both, axis, split_axis=split_dim, concat_axis=concat_dim,...  18 us
    all_to_all x1, blocking collectives, local(): lax.all_to_all(shaped, 'tensor', split_axis=1, concat_axis=1, tiled=True)  17.6 us
    convert_element_type x1, other arithmetic, dequantize(): ((grouped - 8).astype(jnp.float32) * scales[..., None]).astype(jnp.bfloat16)  17.6 us
    all_to_all x1, waiting for transfers between devices, from_everyone(): lax.all_to_all(jnp.broadcast_to(value[None], (size, *value.shape)), axis,...  13.6 us
    all_to_all x3, local copies, waits for them, and re-layouts, side_by_side(): lax.all_to_all(both, axis, split_axis=split_dim, concat_axis=concat_dim,...  13.3 us
  transfers between devices with their start and end apart: 4, of which 4 were waited for; matrix products, arithmetic and copies ran while one was open for 17% of the time, Pallas kernels for 0%

commit v1 on v0

--- a/solution.py
+++ b/solution.py
@@ -94,7 +94,9 @@
         tok_rows, feat_width
     )
     rotated = (mixed_rows * (1.0 / math.sqrt(HB * tensor_size))).astype(jnp.bfloat16)
-    all_tokens = lax.all_gather(rotated, "dp", axis=0, tiled=True)
+    all_tokens = jnp.concatenate(
+        lax.all_to_all(jnp.stack([rotated] * lax.axis_size("dp")), "dp", 0, 0), axis=0
+    )
     store_rows, model_width = weight_codes.shape
     group_count = scale_index.shape[1]
     group_width = model_width // group_count

time: 238 us -> 292 us (1.23)
  waiting for transfers between devices: 81 us -> 129 us
  between operations: 14.3 us -> 0.88 us
  starting transfers between devices: 33.9 us -> 41.3 us
  local copies, waits for them, and re-layouts: 30.9 us -> 37.3 us
  blocking collectives: 53.6 us -> 57.4 us
    all_to_all x0 -> x1, waiting for transfers between devices: none -> 71.6 us  [local(): lax.all_to_all(jnp.stack([rotated] * lax.axis_size('dp')), 'dp', 0, 0)]
    all_gather x1 -> x0, waiting for transfers between devices: 20.7 us -> none  [local(): all_tokens = lax.all_gather(rotated, 'dp', axis=0, tiled=True)]
    all_to_all x0 -> x1, starting transfers between devices: none -> 9.86 us  [local(): lax.all_to_all(jnp.stack([rotated] * lax.axis_size('dp')), 'dp', 0, 0)]
    all_to_all x1, blocking collectives: 36 us -> 39.9 us  [sum_at_owner(): tiles = lax.all_to_all(split_up(value, dim, size), axis, 0, 0, tiled=True)]
    all_to_all x3, local copies, waits for them, and re-layouts: 13.3 us -> 16.6 us  [side_by_side(): lax.all_to_all(both, axis, split_axis=split_dim, concat_axis=concat_dim,...]
    unnamed x14 -> x17, local copies, waits for them, and re-layouts: 7.79 us -> 8 us
  transfers between devices with their start and end apart: 4 -> 4, of which waited for: 4 -> 4; matrix products, arithmetic and copies ran while one was open for 17% -> 16% of each run, Pallas kernels for 0% -> 0%
where the time goes in v1:
time: 292 us; the launch traced here: 291 us
  waiting for transfers between devices  129 us (44%)
  blocking collectives  57.4 us (20%)
  starting transfers between devices  41.3 us (14%)
  local copies, waits for them, and re-layouts  37.3 us (13%)
  other arithmetic  21 us (7%)
  matrix products  3.71 us (1%)
    all_to_all x1, waiting for transfers between devices, local(): lax.all_to_all(jnp.stack([rotated] * lax.axis_size('dp')), 'dp', 0, 0)  71.6 us
    all_to_all x1, waiting for transfers between devices, side_by_side(): lax.all_to_all(both, axis, split_axis=split_dim, concat_axis=concat_dim,...  42.2 us
    all_to_all x1, blocking collectives, sum_at_owner(): tiles = lax.all_to_all(split_up(value, dim, size), axis, 0, 0, tiled=True)  39.9 us
    convert_element_type x1, other arithmetic, dequantize(): ((grouped - 8).astype(jnp.float32) * scales[..., None]).astype(jnp.bfloat16)  18.4 us
    all_to_all x1, starting transfers between devices, side_by_side(): lax.all_to_all(both, axis, split_axis=split_dim, concat_axis=concat_dim,...  18 us
    all_to_all x1, blocking collectives, local(): lax.all_to_all(shaped, 'tensor', split_axis=1, concat_axis=1, tiled=True)  17.6 us
    all_to_all x3, local copies, waits for them, and re-layouts, side_by_side(): lax.all_to_all(both, axis, split_axis=split_dim, concat_axis=concat_dim,...  16.6 us
    all_to_all x1, waiting for transfers between devices, from_everyone(): lax.all_to_all(jnp.broadcast_to(value[None], (size, *value.shape)), axis,...  13.6 us
  transfers between devices with their start and end apart: 4, of which 4 were waited for; matrix products, arithmetic and copies ran while one was open for 16% of the time, Pallas kernels for 0%

profile of v1, /device:TPU:1, one launch (start us, length us, event | category | flops | bytes accessed | tf_op | source)
XLA Modules:
  0.0 290.8 jit_solution(16260657567598703817)
XLA Ops:
  0.6 0.0 copy-start.4
  0.6 1.0 reshape.178
  1.6 0.2 convolution_bitcast_fusion.1
  1.9 0.0 copy-start.3
  1.9 0.2 reshape_reshape.3
  2.1 0.1 copy.92
  2.2 0.0 copy-start.1
  2.2 17.6 %all_to_all.43 = f32[20,16,104]{2,0,1:T(8,128)S(1)} all-to-all(f32[20,16,104]{2,0,1:T(8,128)S(1)} %copy.92), channel_id=1, replica_groups=mesh['dp'=32,'tensor'=16] {'tensor'}, dimensions={1} | all-to-all | bytes 266240 | tf_op jit(solution)/shard_map/all_to_all | solution.py:90
  19.8 0.3 convolution_bitcast_fusion
  20.1 0.7 copy.94
  20.8 4.4 %all-to-all-start.1 = ((f32[20,16,104]{2,0,1:T(8,128)}), f32[20,16,104]{2,0,1:T(8,128)}, u32[]{:S(2)}, u32[]{:S(2)}) async-start(f32[20,16,104]{2,0,1:T(8,128)} %copy.94), calls=%async_computation.1 | async-start | bytes 393216 | tf_op jit(solution)/shard_map/all_to_all | solution.py:93
  25.2 0.0 copy-done.4
  25.2 0.5 copy.98
  25.8 0.0 copy-done.3
  25.8 0.5 copy.97
  26.3 0.0 copy-done.1
  26.3 0.1 convert_element_type.74
  26.4 0.2 copy.111
  26.6 0.1 slice.25
  26.7 0.5 pad_maximum_fusion
  27.3 1.0 copy.133
  28.2 3.5 %reshape.186 = bf16[32,2,6760]{2,1,0:T(2,128)(2,1)} reshape(bf16[64,52,130]{2,1,0:T(8,128)(2,1)S(1)} %bitcast.52) | data formatting | bytes 1730560
  31.8 1.8 all-to-all-done.1
  33.6 18.0 %all-to-all-start.3 = ((bf16[32,2,6760]{2,1,0:T(2,128)(2,1)}), bf16[32,2,6760]{2,1,0:T(2,128)(2,1)S(1)}, u32[]{:S(2)}, u32[]{:S(2)}) async-start(bf16[32,2,6760]{2,1,0:T(2,128)(2,1)} %reshape.186), calls=%async_computation.3 | async-start | bytes 1736704 | tf_op jit(solution)/shard_map/all_to_all | solution.py:16
  51.6 1.0 fusion.16
  52.5 0.2 convert_element_type.73
  52.7 42.2 %all-to-all-done.3 = bf16[32,2,6760]{2,1,0:T(2,128)(2,1)S(1)} async-done(((bf16[32,2,6760]{2,1,0:T(2,128)(2,1)}), bf16[32,2,6760]{2,1,0:T(2,128)(2,1)S(1)}, u32[]{:S(2)}, u32[]{:S(2)}) %all-to-all-start.3) | async-done | bytes 865312 | tf_op jit(solution)/shard_map/all_to_all | solution.py:16
  94.9 1.7 stack.2
  96.5 9.9 %all-to-all-start.2 = ((bf16[32,20,1664]{2,1,0:T(8,128)(2,1)}), bf16[32,20,1664]{2,1,0:T(8,128)(2,1)S(1)}, u32[]{:S(2)}, u32[]{:S(2)}) async-start(bf16[32,20,1664]{2,1,0:T(8,128)(2,1)} %stack.2), calls=%async_computation.2 | async-start | bytes 5111808 | tf_op jit(solution)/shard_map/all_to_all | solution.py:98
  106.4 4.2 %reshape.187 = bf16[64,52,130]{2,1,0:T(8,128)(2,1)} reshape(bf16[32,2,6760]{2,1,0:T(2,128)(2,1)S(1)} %all-to-all-done.3) | data formatting | bytes 1730560
  110.6 4.6 %copy.130 = bf16[52,32,2,130]{3,2,1,0:T(2,128)(2,1)} copy(bf16[52,32,2,130]{3,0,2,1:T(8,128)(2,1)} %bitcast.53) | data formatting | bytes 1730560 | tf_op jit(solution)/shard_map/all_to_all | solution.py:16
  115.2 6.9 %copy.101 = bf16[32,52,2,130]{1,0,3,2:T(8,128)(2,1)} copy(bf16[32,52,2,130]{3,2,0,1:T(2,128)(2,1)} %bitcast.54) | data formatting | bytes 1730560 | tf_op jit(solution)/shard_map/all_to_all | solution.py:16
  122.1 5.1 %all_to_all.34 = bf16[1664,2,130]{0,2,1:T(8,128)(2,1)S(1)} reshape(bf16[32,52,2,130]{1,0,3,2:T(8,128)(2,1)} %copy.101) | data formatting | bytes 1730560 | tf_op jit(solution)/shard_map/all_to_all | solution.py:16
  127.3 0.1 select_reduce_fusion
  127.5 18.4 %fusion.10 = (bf16[1664,2,128]{0,2,1:T(8,128)(2,1)}, bf16[1664,2,128]{0,2,1:T(8,128)(2,1)}) fusion(f32[1664,2]{0,1:T(2,128)S(1)} %select_reduce_fusion, bf16[1664,2,130]{0,2,1:T(8,128)(2,1)S(1)} %all_to_all.34, s32[1664,2]{0,1:T(2,128)S(1)} %get-tuple-element.5, s32[1664,2]{0,1:T(2,128)S(1)} %bitcast.62, s32[1664,2]{0,1:T(2,128)S(1)} %get-tuple-element.4), kind=kLoop, calls=%fused_computation.15 | loop fusion | flops 8093696 | bytes 2609152 | tf_op jit(solution)/shard_map/convert_element_type | solution.py:64
  145.9 2.3 copy.108
  148.2 1.3 copy.107
  149.5 71.6 %all-to-all-done.2 = bf16[32,20,1664]{2,1,0:T(8,128)(2,1)S(1)} async-done(((bf16[32,20,1664]{2,1,0:T(8,128)(2,1)}), bf16[32,20,1664]{2,1,0:T(8,128)(2,1)S(1)}, u32[]{:S(2)}, u32[]{:S(2)}) %all-to-all-start.2) | async-done | bytes 2129952 | tf_op jit(solution)/shard_map/all_to_all | solution.py:98
  221.1 2.1 reshape.183
  223.1 3.2 %fusion = f32[16,40,2,256]{3,1,2,0:T(8,128)S(1)} fusion(bf16[16,40,1664,1]{2,1,0,3:T(8,128)(2,1)} %reshape.183, bf16[1,1664,256]{2,1,0:T(8,128)(2,1)S(1)} %copy-done.2, bf16[1,1664,256]{2,1,0:T(8,128)(2,1)} %copy.107), kind=kOutput, calls=%fused_computation.5 | convolution fusion | flops 1093926912 | bytes 5144576 | tf_op jit(solution)/shard_map/tf,kfd->tkd/dot_general | solution.py:114
  226.3 39.9 %all_to_all.44 = f32[16,40,2,256]{3,1,2,0:T(8,128)S(1)} all-to-all(f32[16,40,2,256]{3,1,2,0:T(8,128)S(1)} %fusion), channel_id=1, replica_groups=mesh['dp'=32,'tensor'=16] {'tensor'}, dimensions={0} | all-to-all | bytes 2621440 | tf_op jit(solution)/shard_map/all_to_all | solution.py:34
  266.1 0.1 reduce_sum.39
  266.2 0.1 fusion.25
  266.3 0.6 broadcast_in_dim.17
  267.0 9.1 %all-to-all-start.5 = ((f32[32,1,40]{2,1,0:T(1,128)}), f32[32,1,40]{2,1,0:T(1,128)S(1)}, u32[]{:S(2)}, u32[]{:S(2)}) async-start(f32[32,1,40]{2,1,0:T(1,128)} %broadcast_in_dim.17), calls=%async_computation.5 | async-start | bytes 32768 | tf_op jit(solution)/shard_map/all_to_all | solution.py:40
  276.0 0.6 fusion.35
  276.6 13.6 %all-to-all-done.5 = f32[32,1,40]{2,1,0:T(1,128)S(1)} async-done(((f32[32,1,40]{2,1,0:T(1,128)}), f32[32,1,40]{2,1,0:T(1,128)S(1)}, u32[]{:S(2)}, u32[]{:S(2)}) %all-to-all-start.5) | async-done | bytes 5152 | tf_op jit(solution)/shard_map/all_to_all | solution.py:40
  290.2 0.5 reduce_sum.41
  (15 shorter events, 0.2 us)
Async XLA Ops:
  0.6 24.6 %copy-start.4 = (s32[1,52,64]{2,0,1:T(1,128)S(1)}, s32[1,52,64]{2,0,1:T(1,128)}, u32[]{:S(2)}) copy-start(s32[1,52,64]{2,0,1:T(1,128)} %param.9) | copy-start | bytes 39940
  1.9 23.9 %copy-start.3 = (s32[52,64]{1,0:T(8,128)S(1)}, s32[52,64]{1,0:T(8,128)}, u32[]{:S(2)}) copy-start(s32[52,64]{1,0:T(8,128)} %param.7) | copy-start | bytes 39940
  2.2 24.1 %copy-start.1 = (s32[52,8192]{1,0:T(8,128)S(1)}, s32[52,8192]{1,0:T(8,128)}, u32[]{:S(2)}) copy-start(s32[52,8192]{1,0:T(8,128)} %param.6) | copy-start | bytes 5111812
  20.8 12.8 %all-to-all-start.1 = ((f32[20,16,104]{2,0,1:T(8,128)}), f32[20,16,104]{2,0,1:T(8,128)}, u32[]{:S(2)}, u32[]{:S(2)}) async-start(f32[20,16,104]{2,0,1:T(8,128)} %copy.94), calls=%async_computation.1 | async-start | bytes 393216 | tf_op jit(solution)/shard_map/all_to_all | solution.py:93
  33.6 61.3 %all-to-all-start.3 = ((bf16[32,2,6760]{2,1,0:T(2,128)(2,1)}), bf16[32,2,6760]{2,1,0:T(2,128)(2,1)S(1)}, u32[]{:S(2)}, u32[]{:S(2)}) async-start(bf16[32,2,6760]{2,1,0:T(2,128)(2,1)} %reshape.186), calls=%async_computation.3 | async-start | bytes 1736704 | tf_op jit(solution)/shard_map/all_to_all | solution.py:16
  96.5 124.5 %all-to-all-start.2 = ((bf16[32,20,1664]{2,1,0:T(8,128)(2,1)}), bf16[32,20,1664]{2,1,0:T(8,128)(2,1)S(1)}, u32[]{:S(2)}, u32[]{:S(2)}) async-start(bf16[32,20,1664]{2,1,0:T(8,128)(2,1)} %stack.2), calls=%async_computation.2 | async-start | bytes 5111808 | tf_op jit(solution)/shard_map/all_to_all | solution.py:98
  122.1 5.2 %copy-start.5 = (f32[16]{0:T(128)S(1)}, f32[16]{0:T(128)}, u32[]{:S(2)}) copy-start(f32[16]{0:T(128)} %param.8) | copy-start | bytes 196
  145.9 2.3 copy-start
  149.5 73.6 %copy-start.2 = (bf16[1,1664,256]{2,1,0:T(8,128)(2,1)S(1)}, bf16[1,1664,256]{2,1,0:T(8,128)(2,1)}, u32[]{:S(2)}) copy-start(bf16[1,1664,256]{2,1,0:T(8,128)(2,1)} %copy.108) | copy-start | bytes 2555908
  267.0 23.3 %all-to-all-start.5 = ((f32[32,1,40]{2,1,0:T(1,128)}), f32[32,1,40]{2,1,0:T(1,128)S(1)}, u32[]{:S(2)}, u32[]{:S(2)}) async-start(f32[32,1,40]{2,1,0:T(1,128)} %broadcast_in_dim.17), calls=%async_computation.5 | async-start | bytes 32768 | tf_op jit(solution)/shard_map/all_to_all | solution.py:40
